TPU v7x, 256 devices: a whole 4x4x8 slice. The times are simulated.
256 devices in a mesh: ctx: 32 (over z, y_lo, core), tp: 8 (over x, y_hi).
Axes of the slice: x: 4, y: 4 (y_hi: 2, y_lo: 2; y = y_hi * 2 + y_lo), z: 8, core: 2. Of those that a mesh axis runs over, the one named last changes fastest.
Arguments:
- queries: bfloat16 [16384, 8192], P('ctx', 'tp'), may hold values from -8 to 8
- stacked_keys: bfloat16 [16384, 1024], P('ctx', 'tp'), may hold values from -8 to 8
- stacked_values: bfloat16 [16384, 1024], P('ctx', 'tp'), may hold values from -6 to 6
- doc_start: int32 [16384], P('ctx'), may hold values from 0 to 16383, as said below
- out_weight: bfloat16 [8192, 4096], P('tp'), may hold values from -0.0625 to 0.0625
Outputs:
- projected: bfloat16 [16384, 4096], P('ctx', 'tp')
Inputs may be any that keep to these rules, and one draw needn't show every extreme that they name: doc_start[t] is the position of the first token of the document holding token t; documents are contiguous runs of 1 to 8192 tokens, one document holds exactly 8192 tokens and does not begin at the first of a device's rows, and the last token forms a document of its own.
All inputs are finite; a program needn't handle non-finite values.
Results may differ from a plain program's by a relative error of at most 0.014.
Values may be sent and summed in bfloat16 or wider, within the bound.
A program may use at most 64 MiB of HBM per device.

v0:
```python
import math

import jax
import jax.numpy as jnp
from jax import lax
from jax.sharding import PartitionSpec as P

HEAD_WIDTH = 128


masked_floor = -1e30


def shifted(block, axis, distance):
    devices = range(lax.axis_size(axis))
    route = [(i - distance, i) for i in devices if i - distance in devices]
    return lax.ppermute(block, axis, route)


def local(queries, stacked_keys, stacked_values, doc_start, out_weight):
    row_count = queries.shape[0]
    kv_local = stacked_keys.shape[1] // HEAD_WIDTH
    queries_per_group = queries.shape[1] // HEAD_WIDTH // kv_local
    score_scale = 1.0 / math.sqrt(HEAD_WIDTH)
    device_index = lax.axis_index("ctx")
    device_row = device_index * row_count
    grouped = queries.reshape(row_count, kv_local, queries_per_group, HEAD_WIDTH)
    query_pos = device_row + jnp.arange(row_count, dtype=jnp.int32)
    earliest = doc_start[0]
    latest = device_row + row_count - 1

    def attend(state, key_tile, value_tile, key_start):
        running_max, running_sum, accum = state
        count = key_tile.shape[0]
        key_heads = key_tile.reshape(count, kv_local, HEAD_WIDTH)
        value_heads = value_tile.reshape(count, kv_local, HEAD_WIDTH)
        scores = (
            jnp.einsum("qhgd,khd->hgqk", grouped, key_heads, preferred_element_type=jnp.float32)
            * score_scale
        )
        key_pos = key_start + jnp.arange(count, dtype=jnp.int32)
        visible = (key_pos[None, :] >= doc_start[:, None]) & (
            key_pos[None, :] <= query_pos[:, None]
        )
        scores = jnp.where(visible, scores, masked_floor)
        new_max = jnp.maximum(running_max, jnp.max(scores, axis=-1))
        rescale = jnp.exp(running_max - new_max)
        weights = jnp.where(visible, jnp.exp(scores - new_max[..., None]), 0.0)
        running_sum = running_sum * rescale + jnp.sum(weights, axis=-1)
        update = jnp.einsum(
            "hgqk,khd->hgqd",
            weights.astype(jnp.bfloat16),
            value_heads,
            preferred_element_type=jnp.float32,
        )
        accum = accum * rescale[..., None] + update
        return (new_max, running_sum, accum)

    def visit(state, key_tile, value_tile, key_start):
        count = key_tile.shape[0]
        needed = (key_start + count - 1 >= earliest) & (key_start <= latest)
        return lax.cond(
            needed,
            lambda inner: attend(inner, key_tile, value_tile, key_start),
            lambda inner: inner,
            state,
        )

    initial = (
        jnp.full((kv_local, queries_per_group, row_count), masked_floor, jnp.float32),
        jnp.zeros((kv_local, queries_per_group, row_count), jnp.float32),
        jnp.zeros((kv_local, queries_per_group, row_count, HEAD_WIDTH), jnp.float32),
    )
    state = attend(initial, stacked_keys, stacked_values, device_row)
    reach = lax.axis_size("ctx") // 2

    def relay_step(distance, carry):
        inner, key_tile, value_tile = carry
        key_tile, value_tile = shifted((key_tile, value_tile), "ctx", 1)
        inner = visit(inner, key_tile, value_tile, (device_index - distance) * row_count)
        return (inner, key_tile, value_tile)

    state, _, _ = lax.fori_loop(1, reach + 1, relay_step, (state, stacked_keys, stacked_values))
    _, running_sum, accum = state
    attended = (accum / running_sum[..., None]).astype(jnp.bfloat16)
    attended = attended.transpose(2, 0, 1, 3).reshape(
        row_count, kv_local * queries_per_group * HEAD_WIDTH
    )
    partial_value = jnp.dot(attended, out_weight, preferred_element_type=jnp.float32)
    return lax.psum_scatter(
        partial_value.astype(jnp.bfloat16), "tp", scatter_dimension=1, tiled=True
    )


def solution(mesh):
    return jax.shard_map(
        local,
        mesh=mesh,
        in_specs=(P("ctx", "tp"), P("ctx", "tp"), P("ctx", "tp"), P("ctx"), P("tp", None)),
        out_specs=P("ctx", "tp"),
        check_vma=False,
    )
```

profile of v0, /device:TPU:2, one launch (start us, length us, event | category | flops | bytes accessed | tf_op | source)
XLA Modules:
  0.0 433.2 jit_solution(12789415363607939592)
XLA Ops:
  21.5 5.0 %add_bitcast_fusion = f32[1,8,512,128]{3,2,1,0:T(8,128)S(1)} fusion(f32[512,512,8]{1,0,2:T(8,128)} %copy-done, f32[8,512]{1,0:T(8,128)S(1)} %get-tuple-element.518, pred[512,512]{0,1:T(8,128)(4,1)S(1)} %compare_and_fusion.1, f32[8,512]{1,0:T(8,128)S(1)} %get-tuple-element.516, bf16[512,128]{1,0:T(8,128)(2,1)} %copy.52), kind=kOutput, calls=%fused_computation.34 | convolution fusion | flops 547880960 | bytes 10911744 | tf_op jit(solution)/shard_map/hgqk,khd->hgqd/dot_general | solution.py:50
  26.6 232.2 %while.26 = (s32[]{:T(128)}, f32[1,8,512]{2,1,0:T(8,128)S(1)}, f32[1,8,512]{2,1,0:T(8,128)S(1)}, f32[1,8,512,128]{3,2,1,0:T(8,128)S(1)}, bf16[512,128]{1,0:T(8,1...) while((s32[]{:T(128)}, f32[1,8,512]{2,1,0:T(8,128)S(1)}, ...), condition=%wide.region_7.8_spmd.clone, body=%wide.region_2.7_spmd.clone.sunk | while | flops 1102853120 | bytes 33569192 | solution.py:83
  34.6 10.0 %collective-permute-start = (bf16[512,128]{1,0:T(8,128)(2,1)}, bf16[512,128]{1,0:T(8,128)(2,1)S(1)}, u32[]{:S(2)}, u32[]{:S(2)}) collective-permute-start(bf16[512,128]{1,0:T(8,128)(2,1)} %get-tuple-element.625), channel_id=1, source_target_pairs={{0,8},{8,16},{16,24},{24,32},{32,40},{40,48},{48,56},{56,64},{64,7... | collective-permute-start | bytes 393224 | tf_op jit(solution)/shard_map/while/body/eval_jaxpr/ppermute | solution.py:17
  44.7 4.2 collective-permute-start.1
  54.4 11.3 %collective-permute-start.1 = (bf16[512,128]{1,0:T(8,128)(2,1)}, bf16[512,128]{1,0:T(8,128)(2,1)S(1)}, u32[]{:S(2)}, u32[]{:S(2)}) collective-permute-start(bf16[512,128]{1,0:T(8,128)(2,1)} %get-tuple-element.626), channel_id=1, source_target_pairs={{0,8},{8,16},{16,24},{24,32},{32,40},{40,48},{48,56},{56,64},{64,7... | collective-permute-start | bytes 393224 | tf_op jit(solution)/shard_map/while/body/eval_jaxpr/ppermute | solution.py:17
  71.1 4.6 %collective-permute-start.1 = (bf16[512,128]{1,0:T(8,128)(2,1)}, bf16[512,128]{1,0:T(8,128)(2,1)S(1)}, u32[]{:S(2)}, u32[]{:S(2)}) collective-permute-start(bf16[512,128]{1,0:T(8,128)(2,1)} %get-tuple-element.626), channel_id=1, source_target_pairs={{0,8},{8,16},{16,24},{24,32},{32,40},{40,48},{48,56},{56,64},{64,7... | collective-permute-start | bytes 393224 | tf_op jit(solution)/shard_map/while/body/eval_jaxpr/ppermute | solution.py:17
  78.2 4.0 collective-permute-start
  82.2 4.2 collective-permute-start.1
  89.0 8.0 %collective-permute-start = (bf16[512,128]{1,0:T(8,128)(2,1)}, bf16[512,128]{1,0:T(8,128)(2,1)S(1)}, u32[]{:S(2)}, u32[]{:S(2)}) collective-permute-start(bf16[512,128]{1,0:T(8,128)(2,1)} %get-tuple-element.625), channel_id=1, source_target_pairs={{0,8},{8,16},{16,24},{24,32},{32,40},{40,48},{48,56},{56,64},{64,7... | collective-permute-start | bytes 393224 | tf_op jit(solution)/shard_map/while/body/eval_jaxpr/ppermute | solution.py:17
  97.0 4.2 collective-permute-start.1
  103.8 3.9 collective-permute-start
  107.6 9.2 %collective-permute-start.1 = (bf16[512,128]{1,0:T(8,128)(2,1)}, bf16[512,128]{1,0:T(8,128)(2,1)S(1)}, u32[]{:S(2)}, u32[]{:S(2)}) collective-permute-start(bf16[512,128]{1,0:T(8,128)(2,1)} %get-tuple-element.626), channel_id=1, source_target_pairs={{0,8},{8,16},{16,24},{24,32},{32,40},{40,48},{48,56},{56,64},{64,7... | collective-permute-start | bytes 393224 | tf_op jit(solution)/shard_map/while/body/eval_jaxpr/ppermute | solution.py:17
  119.3 6.0 %collective-permute-start = (bf16[512,128]{1,0:T(8,128)(2,1)}, bf16[512,128]{1,0:T(8,128)(2,1)S(1)}, u32[]{:S(2)}, u32[]{:S(2)}) collective-permute-start(bf16[512,128]{1,0:T(8,128)(2,1)} %get-tuple-element.625), channel_id=1, source_target_pairs={{0,8},{8,16},{16,24},{24,32},{32,40},{40,48},{48,56},{56,64},{64,7... | collective-permute-start | bytes 393224 | tf_op jit(solution)/shard_map/while/body/eval_jaxpr/ppermute | solution.py:17
  125.3 4.2 collective-permute-start.1
  132.0 10.9 %collective-permute-start = (bf16[512,128]{1,0:T(8,128)(2,1)}, bf16[512,128]{1,0:T(8,128)(2,1)S(1)}, u32[]{:S(2)}, u32[]{:S(2)}) collective-permute-start(bf16[512,128]{1,0:T(8,128)(2,1)} %get-tuple-element.625), channel_id=1, source_target_pairs={{0,8},{8,16},{16,24},{24,32},{32,40},{40,48},{48,56},{56,64},{64,7... | collective-permute-start | bytes 393224 | tf_op jit(solution)/shard_map/while/body/eval_jaxpr/ppermute | solution.py:17
  143.0 4.2 collective-permute-start.1
  149.7 3.9 collective-permute-start
  153.6 9.0 %collective-permute-start.1 = (bf16[512,128]{1,0:T(8,128)(2,1)}, bf16[512,128]{1,0:T(8,128)(2,1)S(1)}, u32[]{:S(2)}, u32[]{:S(2)}) collective-permute-start(bf16[512,128]{1,0:T(8,128)(2,1)} %get-tuple-element.626), channel_id=1, source_target_pairs={{0,8},{8,16},{16,24},{24,32},{32,40},{40,48},{48,56},{56,64},{64,7... | collective-permute-start | bytes 393224 | tf_op jit(solution)/shard_map/while/body/eval_jaxpr/ppermute | solution.py:17
  165.1 6.2 %collective-permute-start = (bf16[512,128]{1,0:T(8,128)(2,1)}, bf16[512,128]{1,0:T(8,128)(2,1)S(1)}, u32[]{:S(2)}, u32[]{:S(2)}) collective-permute-start(bf16[512,128]{1,0:T(8,128)(2,1)} %get-tuple-element.625), channel_id=1, source_target_pairs={{0,8},{8,16},{16,24},{24,32},{32,40},{40,48},{48,56},{56,64},{64,7... | collective-permute-start | bytes 393224 | tf_op jit(solution)/shard_map/while/body/eval_jaxpr/ppermute | solution.py:17
  171.3 4.2 collective-permute-start.1
  178.0 10.0 %collective-permute-start = (bf16[512,128]{1,0:T(8,128)(2,1)}, bf16[512,128]{1,0:T(8,128)(2,1)S(1)}, u32[]{:S(2)}, u32[]{:S(2)}) collective-permute-start(bf16[512,128]{1,0:T(8,128)(2,1)} %get-tuple-element.625), channel_id=1, source_target_pairs={{0,8},{8,16},{16,24},{24,32},{32,40},{40,48},{48,56},{56,64},{64,7... | collective-permute-start | bytes 393224 | tf_op jit(solution)/shard_map/while/body/eval_jaxpr/ppermute | solution.py:17
  188.0 4.2 collective-permute-start.1
  194.7 5.1 %collective-permute-start = (bf16[512,128]{1,0:T(8,128)(2,1)}, bf16[512,128]{1,0:T(8,128)(2,1)S(1)}, u32[]{:S(2)}, u32[]{:S(2)}) collective-permute-start(bf16[512,128]{1,0:T(8,128)(2,1)} %get-tuple-element.625), channel_id=1, source_target_pairs={{0,8},{8,16},{16,24},{24,32},{32,40},{40,48},{48,56},{56,64},{64,7... | collective-permute-start | bytes 393224 | tf_op jit(solution)/shard_map/while/body/eval_jaxpr/ppermute | solution.py:17
  199.8 7.0 %collective-permute-start.1 = (bf16[512,128]{1,0:T(8,128)(2,1)}, bf16[512,128]{1,0:T(8,128)(2,1)S(1)}, u32[]{:S(2)}, u32[]{:S(2)}) collective-permute-start(bf16[512,128]{1,0:T(8,128)(2,1)} %get-tuple-element.626), channel_id=1, source_target_pairs={{0,8},{8,16},{16,24},{24,32},{32,40},{40,48},{48,56},{56,64},{64,7... | collective-permute-start | bytes 393224 | tf_op jit(solution)/shard_map/while/body/eval_jaxpr/ppermute | solution.py:17
  209.4 9.3 %collective-permute-start = (bf16[512,128]{1,0:T(8,128)(2,1)}, bf16[512,128]{1,0:T(8,128)(2,1)S(1)}, u32[]{:S(2)}, u32[]{:S(2)}) collective-permute-start(bf16[512,128]{1,0:T(8,128)(2,1)} %get-tuple-element.625), channel_id=1, source_target_pairs={{0,8},{8,16},{16,24},{24,32},{32,40},{40,48},{48,56},{56,64},{64,7... | collective-permute-start | bytes 393224 | tf_op jit(solution)/shard_map/while/body/eval_jaxpr/ppermute | solution.py:17
  218.7 4.2 collective-permute-start.1
  225.5 12.1 %collective-permute-start = (bf16[512,128]{1,0:T(8,128)(2,1)}, bf16[512,128]{1,0:T(8,128)(2,1)S(1)}, u32[]{:S(2)}, u32[]{:S(2)}) collective-permute-start(bf16[512,128]{1,0:T(8,128)(2,1)} %get-tuple-element.625), channel_id=1, source_target_pairs={{0,8},{8,16},{16,24},{24,32},{32,40},{40,48},{48,56},{56,64},{64,7... | collective-permute-start | bytes 393224 | tf_op jit(solution)/shard_map/while/body/eval_jaxpr/ppermute | solution.py:17
  237.6 4.2 collective-permute-start.1
  244.3 5.1 %collective-permute-start = (bf16[512,128]{1,0:T(8,128)(2,1)}, bf16[512,128]{1,0:T(8,128)(2,1)S(1)}, u32[]{:S(2)}, u32[]{:S(2)}) collective-permute-start(bf16[512,128]{1,0:T(8,128)(2,1)} %get-tuple-element.625), channel_id=1, source_target_pairs={{0,8},{8,16},{16,24},{24,32},{32,40},{40,48},{48,56},{56,64},{64,7... | collective-permute-start | bytes 393224 | tf_op jit(solution)/shard_map/while/body/eval_jaxpr/ppermute | solution.py:17
  249.4 6.9 %collective-permute-start.1 = (bf16[512,128]{1,0:T(8,128)(2,1)}, bf16[512,128]{1,0:T(8,128)(2,1)S(1)}, u32[]{:S(2)}, u32[]{:S(2)}) collective-permute-start(bf16[512,128]{1,0:T(8,128)(2,1)} %get-tuple-element.626), channel_id=1, source_target_pairs={{0,8},{8,16},{16,24},{24,32},{32,40},{40,48},{48,56},{56,64},{64,7... | collective-permute-start | bytes 393224 | tf_op jit(solution)/shard_map/while/body/eval_jaxpr/ppermute | solution.py:17
  262.3 9.5 %convolution_convert_fusion = bf16[512,4096]{1,0:T(8,128)(2,1)} fusion(bf16[512,1024]{0,1:T(8,128)(2,1)S(1)} %bitcast.102, bf16[1024,4096]{1,0:T(8,128)(2,1)} %param.13), kind=kOutput, calls=%fused_computation.27 | convolution fusion | flops 4297064448 | bytes 13631488 | tf_op jit(solution)/shard_map/dot_general | solution.py:89
  271.9 154.5 %reduce-scatter.2.cloned.1.call-done = bf16[512,512]{1,0:T(8,128)(2,1)} async-done(((bf16[512,4096]{1,0:T(8,128)(2,1)}), bf16[512,512]{1,0:T(8,128)(2,1)}) %reduce-scatter.2.cloned.1.call-update) | async-done | bytes 524304 | tf_op jit(solution)/shard_map/reduce_scatter | solution.py:90
  (123 shorter events, 59.3 us)
Async XLA Ops:
  6.5 419.8 %reduce-scatter.2.cloned.1.call-start = ((), (), s32[]{:S(2)}) async-start(), calls=%async_computation.1 | async-start | bytes 4718592 | tf_op jit(solution)/shard_map/reduce_scatter | solution.py:90
  26.6 6.2 %collective-permute-start = (bf16[512,128]{1,0:T(8,128)(2,1)}, bf16[512,128]{1,0:T(8,128)(2,1)S(1)}, u32[]{:S(2)}, u32[]{:S(2)}) collective-permute-start(bf16[512,128]{1,0:T(8,128)(2,1)} %get-tuple-element.625), channel_id=1, source_target_pairs={{0,8},{8,16},{16,24},{24,32},{32,40},{40,48},{48,56},{56,64},{64,7... | collective-permute-start | bytes 393224 | tf_op jit(solution)/shard_map/while/body/eval_jaxpr/ppermute | solution.py:17
  34.6 14.9 %collective-permute-start = (bf16[512,128]{1,0:T(8,128)(2,1)}, bf16[512,128]{1,0:T(8,128)(2,1)S(1)}, u32[]{:S(2)}, u32[]{:S(2)}) collective-permute-start(bf16[512,128]{1,0:T(8,128)(2,1)} %get-tuple-element.625), channel_id=1, source_target_pairs={{0,8},{8,16},{16,24},{24,32},{32,40},{40,48},{48,56},{56,64},{64,7... | collective-permute-start | bytes 393224 | tf_op jit(solution)/shard_map/while/body/eval_jaxpr/ppermute | solution.py:17
  44.7 5.4 %collective-permute-start.1 = (bf16[512,128]{1,0:T(8,128)(2,1)}, bf16[512,128]{1,0:T(8,128)(2,1)S(1)}, u32[]{:S(2)}, u32[]{:S(2)}) collective-permute-start(bf16[512,128]{1,0:T(8,128)(2,1)} %get-tuple-element.626), channel_id=1, source_target_pairs={{0,8},{8,16},{16,24},{24,32},{32,40},{40,48},{48,56},{56,64},{64,7... | collective-permute-start | bytes 393224 | tf_op jit(solution)/shard_map/while/body/eval_jaxpr/ppermute | solution.py:17
  51.4 14.9 %collective-permute-start = (bf16[512,128]{1,0:T(8,128)(2,1)}, bf16[512,128]{1,0:T(8,128)(2,1)S(1)}, u32[]{:S(2)}, u32[]{:S(2)}) collective-permute-start(bf16[512,128]{1,0:T(8,128)(2,1)} %get-tuple-element.625), channel_id=1, source_target_pairs={{0,8},{8,16},{16,24},{24,32},{32,40},{40,48},{48,56},{56,64},{64,7... | collective-permute-start | bytes 393224 | tf_op jit(solution)/shard_map/while/body/eval_jaxpr/ppermute | solution.py:17
  54.4 12.5 %collective-permute-start.1 = (bf16[512,128]{1,0:T(8,128)(2,1)}, bf16[512,128]{1,0:T(8,128)(2,1)S(1)}, u32[]{:S(2)}, u32[]{:S(2)}) collective-permute-start(bf16[512,128]{1,0:T(8,128)(2,1)} %get-tuple-element.626), channel_id=1, source_target_pairs={{0,8},{8,16},{16,24},{24,32},{32,40},{40,48},{48,56},{56,64},{64,7... | collective-permute-start | bytes 393224 | tf_op jit(solution)/shard_map/while/body/eval_jaxpr/ppermute | solution.py:17
  68.2 8.2 %collective-permute-start = (bf16[512,128]{1,0:T(8,128)(2,1)}, bf16[512,128]{1,0:T(8,128)(2,1)S(1)}, u32[]{:S(2)}, u32[]{:S(2)}) collective-permute-start(bf16[512,128]{1,0:T(8,128)(2,1)} %get-tuple-element.625), channel_id=1, source_target_pairs={{0,8},{8,16},{16,24},{24,32},{32,40},{40,48},{48,56},{56,64},{64,7... | collective-permute-start | bytes 393224 | tf_op jit(solution)/shard_map/while/body/eval_jaxpr/ppermute | solution.py:17
  71.1 5.7 %collective-permute-start.1 = (bf16[512,128]{1,0:T(8,128)(2,1)}, bf16[512,128]{1,0:T(8,128)(2,1)S(1)}, u32[]{:S(2)}, u32[]{:S(2)}) collective-permute-start(bf16[512,128]{1,0:T(8,128)(2,1)} %get-tuple-element.626), channel_id=1, source_target_pairs={{0,8},{8,16},{16,24},{24,32},{32,40},{40,48},{48,56},{56,64},{64,7... | collective-permute-start | bytes 393224 | tf_op jit(solution)/shard_map/while/body/eval_jaxpr/ppermute | solution.py:17
  78.2 8.9 %collective-permute-start = (bf16[512,128]{1,0:T(8,128)(2,1)}, bf16[512,128]{1,0:T(8,128)(2,1)S(1)}, u32[]{:S(2)}, u32[]{:S(2)}) collective-permute-start(bf16[512,128]{1,0:T(8,128)(2,1)} %get-tuple-element.625), channel_id=1, source_target_pairs={{0,8},{8,16},{16,24},{24,32},{32,40},{40,48},{48,56},{56,64},{64,7... | collective-permute-start | bytes 393224 | tf_op jit(solution)/shard_map/while/body/eval_jaxpr/ppermute | solution.py:17
  82.2 5.4 %collective-permute-start.1 = (bf16[512,128]{1,0:T(8,128)(2,1)}, bf16[512,128]{1,0:T(8,128)(2,1)S(1)}, u32[]{:S(2)}, u32[]{:S(2)}) collective-permute-start(bf16[512,128]{1,0:T(8,128)(2,1)} %get-tuple-element.626), channel_id=1, source_target_pairs={{0,8},{8,16},{16,24},{24,32},{32,40},{40,48},{48,56},{56,64},{64,7... | collective-permute-start | bytes 393224 | tf_op jit(solution)/shard_map/while/body/eval_jaxpr/ppermute | solution.py:17
  89.0 12.9 %collective-permute-start = (bf16[512,128]{1,0:T(8,128)(2,1)}, bf16[512,128]{1,0:T(8,128)(2,1)S(1)}, u32[]{:S(2)}, u32[]{:S(2)}) collective-permute-start(bf16[512,128]{1,0:T(8,128)(2,1)} %get-tuple-element.625), channel_id=1, source_target_pairs={{0,8},{8,16},{16,24},{24,32},{32,40},{40,48},{48,56},{56,64},{64,7... | collective-permute-start | bytes 393224 | tf_op jit(solution)/shard_map/while/body/eval_jaxpr/ppermute | solution.py:17
  97.0 5.4 %collective-permute-start.1 = (bf16[512,128]{1,0:T(8,128)(2,1)}, bf16[512,128]{1,0:T(8,128)(2,1)S(1)}, u32[]{:S(2)}, u32[]{:S(2)}) collective-permute-start(bf16[512,128]{1,0:T(8,128)(2,1)} %get-tuple-element.626), channel_id=1, source_target_pairs={{0,8},{8,16},{16,24},{24,32},{32,40},{40,48},{48,56},{56,64},{64,7... | collective-permute-start | bytes 393224 | tf_op jit(solution)/shard_map/while/body/eval_jaxpr/ppermute | solution.py:17
  103.8 13.7 %collective-permute-start = (bf16[512,128]{1,0:T(8,128)(2,1)}, bf16[512,128]{1,0:T(8,128)(2,1)S(1)}, u32[]{:S(2)}, u32[]{:S(2)}) collective-permute-start(bf16[512,128]{1,0:T(8,128)(2,1)} %get-tuple-element.625), channel_id=1, source_target_pairs={{0,8},{8,16},{16,24},{24,32},{32,40},{40,48},{48,56},{56,64},{64,7... | collective-permute-start | bytes 393224 | tf_op jit(solution)/shard_map/while/body/eval_jaxpr/ppermute | solution.py:17
  107.6 10.3 %collective-permute-start.1 = (bf16[512,128]{1,0:T(8,128)(2,1)}, bf16[512,128]{1,0:T(8,128)(2,1)S(1)}, u32[]{:S(2)}, u32[]{:S(2)}) collective-permute-start(bf16[512,128]{1,0:T(8,128)(2,1)} %get-tuple-element.626), channel_id=1, source_target_pairs={{0,8},{8,16},{16,24},{24,32},{32,40},{40,48},{48,56},{56,64},{64,7... | collective-permute-start | bytes 393224 | tf_op jit(solution)/shard_map/while/body/eval_jaxpr/ppermute | solution.py:17
  119.3 10.9 %collective-permute-start = (bf16[512,128]{1,0:T(8,128)(2,1)}, bf16[512,128]{1,0:T(8,128)(2,1)S(1)}, u32[]{:S(2)}, u32[]{:S(2)}) collective-permute-start(bf16[512,128]{1,0:T(8,128)(2,1)} %get-tuple-element.625), channel_id=1, source_target_pairs={{0,8},{8,16},{16,24},{24,32},{32,40},{40,48},{48,56},{56,64},{64,7... | collective-permute-start | bytes 393224 | tf_op jit(solution)/shard_map/while/body/eval_jaxpr/ppermute | solution.py:17
  125.3 5.4 %collective-permute-start.1 = (bf16[512,128]{1,0:T(8,128)(2,1)}, bf16[512,128]{1,0:T(8,128)(2,1)S(1)}, u32[]{:S(2)}, u32[]{:S(2)}) collective-permute-start(bf16[512,128]{1,0:T(8,128)(2,1)} %get-tuple-element.626), channel_id=1, source_target_pairs={{0,8},{8,16},{16,24},{24,32},{32,40},{40,48},{48,56},{56,64},{64,7... | collective-permute-start | bytes 393224 | tf_op jit(solution)/shard_map/while/body/eval_jaxpr/ppermute | solution.py:17
  132.0 15.8 %collective-permute-start = (bf16[512,128]{1,0:T(8,128)(2,1)}, bf16[512,128]{1,0:T(8,128)(2,1)S(1)}, u32[]{:S(2)}, u32[]{:S(2)}) collective-permute-start(bf16[512,128]{1,0:T(8,128)(2,1)} %get-tuple-element.625), channel_id=1, source_target_pairs={{0,8},{8,16},{16,24},{24,32},{32,40},{40,48},{48,56},{56,64},{64,7... | collective-permute-start | bytes 393224 | tf_op jit(solution)/shard_map/while/body/eval_jaxpr/ppermute | solution.py:17
  143.0 5.4 %collective-permute-start.1 = (bf16[512,128]{1,0:T(8,128)(2,1)}, bf16[512,128]{1,0:T(8,128)(2,1)S(1)}, u32[]{:S(2)}, u32[]{:S(2)}) collective-permute-start(bf16[512,128]{1,0:T(8,128)(2,1)} %get-tuple-element.626), channel_id=1, source_target_pairs={{0,8},{8,16},{16,24},{24,32},{32,40},{40,48},{48,56},{56,64},{64,7... | collective-permute-start | bytes 393224 | tf_op jit(solution)/shard_map/while/body/eval_jaxpr/ppermute | solution.py:17
  149.7 13.5 %collective-permute-start = (bf16[512,128]{1,0:T(8,128)(2,1)}, bf16[512,128]{1,0:T(8,128)(2,1)S(1)}, u32[]{:S(2)}, u32[]{:S(2)}) collective-permute-start(bf16[512,128]{1,0:T(8,128)(2,1)} %get-tuple-element.625), channel_id=1, source_target_pairs={{0,8},{8,16},{16,24},{24,32},{32,40},{40,48},{48,56},{56,64},{64,7... | collective-permute-start | bytes 393224 | tf_op jit(solution)/shard_map/while/body/eval_jaxpr/ppermute | solution.py:17
  153.6 10.2 %collective-permute-start.1 = (bf16[512,128]{1,0:T(8,128)(2,1)}, bf16[512,128]{1,0:T(8,128)(2,1)S(1)}, u32[]{:S(2)}, u32[]{:S(2)}) collective-permute-start(bf16[512,128]{1,0:T(8,128)(2,1)} %get-tuple-element.626), channel_id=1, source_target_pairs={{0,8},{8,16},{16,24},{24,32},{32,40},{40,48},{48,56},{56,64},{64,7... | collective-permute-start | bytes 393224 | tf_op jit(solution)/shard_map/while/body/eval_jaxpr/ppermute | solution.py:17
  165.1 11.1 %collective-permute-start = (bf16[512,128]{1,0:T(8,128)(2,1)}, bf16[512,128]{1,0:T(8,128)(2,1)S(1)}, u32[]{:S(2)}, u32[]{:S(2)}) collective-permute-start(bf16[512,128]{1,0:T(8,128)(2,1)} %get-tuple-element.625), channel_id=1, source_target_pairs={{0,8},{8,16},{16,24},{24,32},{32,40},{40,48},{48,56},{56,64},{64,7... | collective-permute-start | bytes 393224 | tf_op jit(solution)/shard_map/while/body/eval_jaxpr/ppermute | solution.py:17
  171.3 5.4 %collective-permute-start.1 = (bf16[512,128]{1,0:T(8,128)(2,1)}, bf16[512,128]{1,0:T(8,128)(2,1)S(1)}, u32[]{:S(2)}, u32[]{:S(2)}) collective-permute-start(bf16[512,128]{1,0:T(8,128)(2,1)} %get-tuple-element.626), channel_id=1, source_target_pairs={{0,8},{8,16},{16,24},{24,32},{32,40},{40,48},{48,56},{56,64},{64,7... | collective-permute-start | bytes 393224 | tf_op jit(solution)/shard_map/while/body/eval_jaxpr/ppermute | solution.py:17
  178.0 14.9 %collective-permute-start = (bf16[512,128]{1,0:T(8,128)(2,1)}, bf16[512,128]{1,0:T(8,128)(2,1)S(1)}, u32[]{:S(2)}, u32[]{:S(2)}) collective-permute-start(bf16[512,128]{1,0:T(8,128)(2,1)} %get-tuple-element.625), channel_id=1, source_target_pairs={{0,8},{8,16},{16,24},{24,32},{32,40},{40,48},{48,56},{56,64},{64,7... | collective-permute-start | bytes 393224 | tf_op jit(solution)/shard_map/while/body/eval_jaxpr/ppermute | solution.py:17
  188.0 5.4 %collective-permute-start.1 = (bf16[512,128]{1,0:T(8,128)(2,1)}, bf16[512,128]{1,0:T(8,128)(2,1)S(1)}, u32[]{:S(2)}, u32[]{:S(2)}) collective-permute-start(bf16[512,128]{1,0:T(8,128)(2,1)} %get-tuple-element.626), channel_id=1, source_target_pairs={{0,8},{8,16},{16,24},{24,32},{32,40},{40,48},{48,56},{56,64},{64,7... | collective-permute-start | bytes 393224 | tf_op jit(solution)/shard_map/while/body/eval_jaxpr/ppermute | solution.py:17
  194.7 12.8 %collective-permute-start = (bf16[512,128]{1,0:T(8,128)(2,1)}, bf16[512,128]{1,0:T(8,128)(2,1)S(1)}, u32[]{:S(2)}, u32[]{:S(2)}) collective-permute-start(bf16[512,128]{1,0:T(8,128)(2,1)} %get-tuple-element.625), channel_id=1, source_target_pairs={{0,8},{8,16},{16,24},{24,32},{32,40},{40,48},{48,56},{56,64},{64,7... | collective-permute-start | bytes 393224 | tf_op jit(solution)/shard_map/while/body/eval_jaxpr/ppermute | solution.py:17
  199.8 8.2 %collective-permute-start.1 = (bf16[512,128]{1,0:T(8,128)(2,1)}, bf16[512,128]{1,0:T(8,128)(2,1)S(1)}, u32[]{:S(2)}, u32[]{:S(2)}) collective-permute-start(bf16[512,128]{1,0:T(8,128)(2,1)} %get-tuple-element.626), channel_id=1, source_target_pairs={{0,8},{8,16},{16,24},{24,32},{32,40},{40,48},{48,56},{56,64},{64,7... | collective-permute-start | bytes 393224 | tf_op jit(solution)/shard_map/while/body/eval_jaxpr/ppermute | solution.py:17
  209.4 14.2 %collective-permute-start = (bf16[512,128]{1,0:T(8,128)(2,1)}, bf16[512,128]{1,0:T(8,128)(2,1)S(1)}, u32[]{:S(2)}, u32[]{:S(2)}) collective-permute-start(bf16[512,128]{1,0:T(8,128)(2,1)} %get-tuple-element.625), channel_id=1, source_target_pairs={{0,8},{8,16},{16,24},{24,32},{32,40},{40,48},{48,56},{56,64},{64,7... | collective-permute-start | bytes 393224 | tf_op jit(solution)/shard_map/while/body/eval_jaxpr/ppermute | solution.py:17
  218.7 5.4 %collective-permute-start.1 = (bf16[512,128]{1,0:T(8,128)(2,1)}, bf16[512,128]{1,0:T(8,128)(2,1)S(1)}, u32[]{:S(2)}, u32[]{:S(2)}) collective-permute-start(bf16[512,128]{1,0:T(8,128)(2,1)} %get-tuple-element.626), channel_id=1, source_target_pairs={{0,8},{8,16},{16,24},{24,32},{32,40},{40,48},{48,56},{56,64},{64,7... | collective-permute-start | bytes 393224 | tf_op jit(solution)/shard_map/while/body/eval_jaxpr/ppermute | solution.py:17
  225.5 17.0 %collective-permute-start = (bf16[512,128]{1,0:T(8,128)(2,1)}, bf16[512,128]{1,0:T(8,128)(2,1)S(1)}, u32[]{:S(2)}, u32[]{:S(2)}) collective-permute-start(bf16[512,128]{1,0:T(8,128)(2,1)} %get-tuple-element.625), channel_id=1, source_target_pairs={{0,8},{8,16},{16,24},{24,32},{32,40},{40,48},{48,56},{56,64},{64,7... | collective-permute-start | bytes 393224 | tf_op jit(solution)/shard_map/while/body/eval_jaxpr/ppermute | solution.py:17
  237.6 5.4 %collective-permute-start.1 = (bf16[512,128]{1,0:T(8,128)(2,1)}, bf16[512,128]{1,0:T(8,128)(2,1)S(1)}, u32[]{:S(2)}, u32[]{:S(2)}) collective-permute-start(bf16[512,128]{1,0:T(8,128)(2,1)} %get-tuple-element.626), channel_id=1, source_target_pairs={{0,8},{8,16},{16,24},{24,32},{32,40},{40,48},{48,56},{56,64},{64,7... | collective-permute-start | bytes 393224 | tf_op jit(solution)/shard_map/while/body/eval_jaxpr/ppermute | solution.py:17
  244.3 12.6 %collective-permute-start = (bf16[512,128]{1,0:T(8,128)(2,1)}, bf16[512,128]{1,0:T(8,128)(2,1)S(1)}, u32[]{:S(2)}, u32[]{:S(2)}) collective-permute-start(bf16[512,128]{1,0:T(8,128)(2,1)} %get-tuple-element.625), channel_id=1, source_target_pairs={{0,8},{8,16},{16,24},{24,32},{32,40},{40,48},{48,56},{56,64},{64,7... | collective-permute-start | bytes 393224 | tf_op jit(solution)/shard_map/while/body/eval_jaxpr/ppermute | solution.py:17
  249.4 8.0 %collective-permute-start.1 = (bf16[512,128]{1,0:T(8,128)(2,1)}, bf16[512,128]{1,0:T(8,128)(2,1)S(1)}, u32[]{:S(2)}, u32[]{:S(2)}) collective-permute-start(bf16[512,128]{1,0:T(8,128)(2,1)} %get-tuple-element.626), channel_id=1, source_target_pairs={{0,8},{8,16},{16,24},{24,32},{32,40},{40,48},{48,56},{56,64},{64,7... | collective-permute-start | bytes 393224 | tf_op jit(solution)/shard_map/while/body/eval_jaxpr/ppermute | solution.py:17
  (5 other events, 27.9 us)
Sparse Core Ops, SparseCore 0:
  272.0 154.3 reduce-scatter.1
where the time goes:
time: 430 us; the launch traced here: 433 us
  starting transfers between devices  192 us (45%)
  waiting for transfers between devices  163 us (38%)
  local copies, waits for them, and re-layouts  33.3 us (8%)
  matrix products  17.3 us (4%)
  between operations  13.5 us (3%)
  loops' own time  10.6 us (2%)
    ppermute x32, starting transfers between devices, shifted(): return lax.ppermute(block, axis, route)  192 us
    reduce_scatter x1, waiting for transfers between devices, local(): lax.psum_scatter(partial_value.astype(jnp.bfloat16), 'tp', scatter_dimens...  154 us
    while x32, local copies, waits for them, and re-layouts  20.9 us
    another operation x1, loops' own time, local(): lax.fori_loop(1, reach + 1, relay_step, (state, stacked_keys, stacked_val...  10.6 us
    dot_general x1, matrix products, local(): jnp.dot(attended, out_weight, preferred_element_type=jnp.float32)  9.5 us
    unnamed x12, local copies, waits for them, and re-layouts  9.21 us
  transfers between devices with their start and end apart: 33, of which 17 were waited for; matrix products, arithmetic and copies ran while one was open for 0% of the time, Pallas kernels for 0%

commit v1 on v0

v1 whole, which is shorter than its diff:
```python
import functools
import math

import jax
import jax.numpy as jnp
from jax import lax
from jax.experimental import pallas as pl
from jax.experimental.pallas import tpu as pltpu

HEAD = 128
HEADS = 8
ROWS = 512
CHUNK = 128
CHUNKS = ROWS // CHUNK
WIDE = CHUNK * HEADS
PAIR = 2 * ROWS
VROWS = 144
ACC = 136
COLS = 512
TAIL = 4
SCALE = math.log2(math.e) / math.sqrt(HEAD)
BIG = 1e30
BF16 = jnp.bfloat16
F32 = jnp.float32
MESH = pl.DeviceIdType.MESH


def kernel(q_hbm, k_ref, v_ref, ds_ref, w_hbm, out_ref, q_buf, w_buf, qs, k_own, v_own, v_raw, kb, vb,
           s_buf, m_ref, acc, att, part, ra, rb, cb, rc, fb, local_sem, kv_send, kv_recv, rs_send, rs_recv):
    i = lax.axis_index("ctx")
    t = lax.axis_index("tp")
    z = i // 4
    yl = (i // 2) % 2
    c = i % 2
    x = t // 2
    yh = t % 2
    z_next = {"ctx": (i + 4) % 32}
    z_prev = {"ctx": (i + 28) % 32}
    core = {"ctx": i + 1 - 2 * c}
    y_mate = {"ctx": i + 2 - 4 * yl}
    x_next = {"tp": (t + 2) % 8}
    x_prev = {"tp": (t + 6) % 8}
    yh_mate = {"tp": t + 1 - 2 * yh}

    load_q = pltpu.make_async_copy(q_hbm, q_buf, local_sem.at[0])
    load_w = pltpu.make_async_copy(w_hbm, w_buf, local_sem.at[1])
    load_q.start()
    load_w.start()

    barrier = pltpu.get_barrier_semaphore()
    for mate in (z_next, z_prev, core, y_mate, x_next, x_prev, yh_mate):
        pl.semaphore_signal(barrier, inc=1, device_id=mate, device_id_type=MESH)

    last = ds_ref[CHUNKS - 1:CHUNKS, CHUNK - 1:CHUNK] - i * ROWS
    kf = k_ref[...].astype(F32)
    keep_rows = lax.broadcasted_iota(jnp.int32, (ROWS, HEAD), 0) >= last
    k_own[...] = jnp.where(keep_rows, kf, kf[ROWS - 1:ROWS, :]).astype(BF16)
    vt = v_ref[...].T
    keep_cols = lax.broadcasted_iota(jnp.int32, (HEAD, ROWS), 1) >= last
    v_own[0:HEAD, :] = jnp.where(keep_cols, vt.astype(F32), 0.0).astype(BF16)
    v_own[HEAD:VROWS, :] = jnp.where(keep_cols[0:VROWS - HEAD, :], 1.0, 0.0).astype(BF16)
    v_raw[0:HEAD, :] = vt
    v_raw[HEAD:VROWS, :] = jnp.ones((VROWS - HEAD, ROWS), BF16)

    pl.semaphore_wait(barrier, 7)

    def half(slot, h):
        off = pl.multiple_of(h * ROWS, ROWS)
        return kb.at[slot, pl.ds(off, ROWS), :], vb.at[slot, :, pl.ds(off, ROWS)]

    def message(src, slot, h, number, mate):
        dst = half(slot, h)
        return [
            pltpu.make_async_remote_copy(
                src_ref=src[n], dst_ref=dst[n], send_sem=kv_send.at[2 * number + n],
                recv_sem=kv_recv.at[2 * number + n], device_id=mate, device_id_type=MESH)
            for n in range(2)
        ]

    def send(src, slot, h, number, mate):
        for copy in message(src, slot, h, number, mate):
            copy.start()

    def arrived(slot, h, number):
        for copy in message(half(slot, h), slot, h, number, core):
            copy.wait_recv()

    own = (k_own, v_own)
    send(own, yl, c, 0, z_next)

    @pl.when(yl == 0)
    def _():
        send(own, 7, c, 11, y_mate)

    @pl.when(c == 0)
    def _():
        send(own, 6, 0, 7, core)

    def relay(dz):
        if dz == 4:
            arrived(6, c, 3)

            @pl.when(c == 1)
            def _():
                send(half(6, 1), 6, 1, 7, core)

            @pl.when(yl == 1)
            def _():
                send(half(6, c), 7, c, 11, y_mate)
            return
        slot = 2 * (dz - 1) + yl
        arrived(slot, c, dz - 1)
        src = half(slot, c)
        send(src, 6 if dz == 3 else slot + 2, c, dz, z_next)
        send(src, slot, c, 3 + dz, core)
        send(src, slot, c, 7 + dz, y_mate)

    def relay_y(dz):
        slot = 7 if dz == 4 else 2 * (dz - 1) + 1 - yl
        arrived(slot, c, 7 + dz)
        send(half(slot, c), slot, c, 11 + dz, core)

    def ready(step):
        if step == 6:
            arrived(6, 1 - c, 7)
        elif step == 7:
            arrived(7, 1 - c, 15)
        elif step % 2 == 0:
            arrived(step + yl, 1 - c, 4 + step // 2)
        else:
            arrived(step - yl, 1 - c, 12 + step // 2)

    def slot_of(step):
        b = step % 2
        return (step // 2) * 2 + yl + b - 2 * yl * b

    def ends_of(step):
        b = step % 2
        block = (z - 1 - step // 2) * 4 + 2 * (yl + b - 2 * yl * b)
        return block * ROWS + ROWS - 1, block * ROWS + 2 * ROWS - 1

    ends_6 = ((i - c) * ROWS - 16 * ROWS * (1 - c) + ROWS - 1, (i - c + 1 - 16) * ROWS + ROWS - 1)
    block_7 = z * 4 * yl + (z * 4 - 14) * (1 - yl)
    ends_7 = (block_7 * ROWS + ROWS - 1, block_7 * ROWS + 2 * ROWS - 1)

    def wide(row):
        return jnp.concatenate([row] * HEADS, axis=1)

    load_q.wait()
    for r in range(CHUNKS):
        for h in range(HEADS):
            scaled = q_buf[r * CHUNK:(r + 1) * CHUNK, h * HEAD:(h + 1) * HEAD].astype(F32) * SCALE
            high = scaled.astype(BF16)
            low = (scaled - high.astype(F32)).astype(BF16)
            rows = slice(r * WIDE + h * HEAD, r * WIDE + (h + 1) * HEAD)
            qs[rows, 0:HEAD] = high
            qs[rows, HEAD:2 * HEAD] = low

    def products(keys, r):
        rows = pl.ds(pl.multiple_of(r * WIDE, WIDE), WIDE)
        return lax.dot_general(jnp.concatenate([keys, keys], axis=1), qs[rows, :],
                               (((1,), (1,)), ((), ())), preferred_element_type=F32)

    for r in range(CHUNKS):
        count = (r + 1) * CHUNK
        cols = slice(r * WIDE, (r + 1) * WIDE)
        s = products(k_ref[0:count, :], r)
        key_at = lax.broadcasted_iota(jnp.int32, (count, CHUNK), 0)
        query_at = lax.broadcasted_iota(jnp.int32, (count, CHUNK), 1) + r * CHUNK
        visible = (key_at >= ds_ref[r:r + 1, :] - i * ROWS) & (key_at <= query_at)
        s = jnp.where(jnp.concatenate([visible] * HEADS, axis=1), s, -BIG)
        m = jnp.max(s, axis=0, keepdims=True)
        p = jnp.exp2(s - m).astype(BF16)
        m_ref[:, cols] = m
        acc[:, cols] = jnp.dot(v_raw[0:ACC, 0:count], p, preferred_element_type=F32)

    def scores(slot, r, b):
        s_buf[b] = products(kb[slot], r)

    def update(slot, r, b, ends):
        cols = pl.ds(pl.multiple_of(r * WIDE, WIDE), WIDE)
        starts = ds_ref[pl.ds(r, 1), :]
        off0 = wide(jnp.where(starts <= ends[0], 0.0, BIG))
        off1 = wide(jnp.where(starts <= ends[1], 0.0, BIG))
        s0 = s_buf[b, 0:ROWS, :]
        s1 = s_buf[b, ROWS:PAIR, :]
        m_old = m_ref[:, cols]
        top = jnp.maximum(jnp.max(s0, axis=0, keepdims=True) - off0, jnp.max(s1, axis=0, keepdims=True) - off1)
        m = jnp.maximum(m_old, top)
        m_ref[:, cols] = m
        p0 = jnp.exp2(s0 - (m + off0)).astype(BF16)
        p1 = jnp.exp2(s1 - (m + off1)).astype(BF16)
        p = jnp.concatenate([p0, p1], axis=0)
        new = jnp.dot(vb[slot, 0:ACC, :], p, preferred_element_type=F32)
        acc[:, cols] = acc[:, cols] * jnp.exp2(m_old - m) + new

    relay(1)
    ready(0)
    scores(slot_of(0), 0, 0)

    steps = 8 - TAIL

    @pl.loop(0, 2 * steps)
    def _(hs):
        step = hs // 2
        odd = hs % 2

        for n in range(steps):
            @pl.when(hs == 2 * n + 1)
            def _(n=n):
                if n <= 3:
                    relay_y(n + 1)
                if n <= 2:
                    relay(n + 2)
                ready(n + 1)

        slot = slot_of(step)
        ends = ends_of(step)
        scores(slot, 2 * odd + 1, 1)
        update(slot, 2 * odd, 0, ends)
        scores(slot_of(step + odd), 2 - 2 * odd, 0)
        update(slot, 2 * odd + 1, 1, ends)

    def tail_step(step):
        if step == 6:
            return 6, ends_6
        if step == 7:
            return 7, ends_7
        return slot_of(step), ends_of(step)

    def rs_copy(src, dst, number, mate):
        return pltpu.make_async_remote_copy(
            src_ref=src, dst_ref=dst, send_sem=rs_send.at[number], recv_sem=rs_recv.at[number],
            device_id=mate, device_id_type=MESH)

    far = (x + 2) % 4
    after = (x + 1) % 4
    before = (x + 3) % 4

    def first(r):
        return (rs_copy(part.at[r, 2 * far + 1], ra.at[r, 0], 5 * r, x_next),
                rs_copy(part.at[r, 2 * far], ra.at[r, 1], 5 * r + 1, x_prev))

    def second(r):
        return (rs_copy(part.at[r, pl.ds(2 * after, 2)], rb.at[r, 0], 5 * r + 2, x_next),
                rs_copy(part.at[r, pl.ds(2 * before, 2)], rb.at[r, 1], 5 * r + 3, x_prev))

    def third(r):
        return rs_copy(cb.at[r], rc.at[r], 5 * r + 4, yh_mate)

    def pass_first(r):
        got = first(r)
        onward = second(r)
        for n, block in ((0, 2 * after + 1), (1, 2 * before)):
            got[n].wait_recv()
            part[r, block] = (part[r, block].astype(F32) + ra[r, n].astype(F32)).astype(BF16)
            onward[n].start()

    def pass_second(r):
        for copy in second(r):
            copy.wait_recv()
        for keep in range(2):
            block = yh if keep else 1 - yh
            total = (part[r, 2 * x + block].astype(F32) + rb[r, 0, block].astype(F32)
                     + rb[r, 1, block].astype(F32))
            if keep:
                fb[r] = total
            else:
                cb[r] = total.astype(BF16)
                third(r).start()

    def pass_third(r):
        third(r).wait_recv()
        rows = pl.ds(pl.multiple_of(r * CHUNK, CHUNK), CHUNK)
        out_ref[rows, :] = (fb[r] + rc[r].astype(F32)).astype(BF16)

    load_w.wait()

    @pl.loop(0, CHUNKS)
    def _(r):
        for n in range(TAIL):
            step = 8 - TAIL + n
            if n < TAIL - 1:
                @pl.when(r == 0)
                def _():
                    ready(step + 1)
                scores(tail_step(step + 1)[0], r, (n + 1) % 2)
            else:
                scores(tail_step(8 - TAIL)[0], (r + 1) % CHUNKS, 0)
            slot, ends = tail_step(step)
            update(slot, r, n % 2, ends)

        @pl.when(r >= 1)
        def _():
            pass_first(r - 1)

        cols = pl.ds(pl.multiple_of(r * WIDE, WIDE), WIDE)
        done = (acc[0:HEAD, cols] / acc[HEAD:HEAD + 1, cols]).astype(BF16)
        for h in range(HEADS):
            att[:, h * HEAD:(h + 1) * HEAD] = done[:, h * CHUNK:(h + 1) * CHUNK].T
        for block in range(8):
            part[r, block] = jnp.dot(att[...], w_buf[:, block * COLS:(block + 1) * COLS],
                                     preferred_element_type=F32).astype(BF16)
        for copy in first(r):
            copy.start()

        @pl.when(r >= 2)
        def _():
            pass_second(r - 2)

    pass_first(CHUNKS - 1)
    pass_second(CHUNKS - 2)
    pass_third(0)
    pass_third(1)
    pass_second(CHUNKS - 1)
    pass_third(2)
    pass_third(3)

    for number in range(16):
        for copy in message(own, 0, 0, number, core):
            copy.wait_send()
    for r in range(CHUNKS):
        for copy in (*first(r), *second(r), third(r)):
            copy.wait_send()


def local(queries, stacked_keys, stacked_values, doc_start, out_weight):
    vmem = pl.BlockSpec(memory_space=pltpu.VMEM)
    anywhere = pl.BlockSpec(memory_space=pl.ANY)
    return pl.pallas_call(
        kernel,
        out_shape=jax.ShapeDtypeStruct((ROWS, COLS), BF16),
        in_specs=[anywhere, vmem, vmem, vmem, anywhere],
        out_specs=vmem,
        scratch_shapes=[
            pltpu.VMEM((ROWS, HEADS * HEAD), BF16),
            pltpu.VMEM((HEADS * HEAD, 8 * COLS), BF16),
            pltpu.VMEM((CHUNKS * WIDE, 2 * HEAD), BF16),
            pltpu.VMEM((ROWS, HEAD), BF16),
            pltpu.VMEM((VROWS, ROWS), BF16),
            pltpu.VMEM((VROWS, ROWS), BF16),
            pltpu.VMEM((8, PAIR, HEAD), BF16),
            pltpu.VMEM((8, VROWS, PAIR), BF16),
            pltpu.VMEM((2, PAIR, WIDE), F32),
            pltpu.VMEM((1, CHUNKS * WIDE), F32),
            pltpu.VMEM((ACC, CHUNKS * WIDE), F32),
            pltpu.VMEM((CHUNK, HEADS * HEAD), BF16),
            pltpu.VMEM((CHUNKS, 8, CHUNK, COLS), BF16),
            pltpu.VMEM((CHUNKS, 2, CHUNK, COLS), BF16),
            pltpu.VMEM((CHUNKS, 2, 2, CHUNK, COLS), BF16),
            pltpu.VMEM((CHUNKS, CHUNK, COLS), BF16),
            pltpu.VMEM((CHUNKS, CHUNK, COLS), BF16),
            pltpu.VMEM((CHUNKS, CHUNK, COLS), F32),
            pltpu.SemaphoreType.DMA((2,)),
            pltpu.SemaphoreType.DMA((32,)),
            pltpu.SemaphoreType.DMA((32,)),
            pltpu.SemaphoreType.DMA((5 * CHUNKS,)),
            pltpu.SemaphoreType.DMA((5 * CHUNKS,)),
        ],
        compiler_params=pltpu.CompilerParams(
            collective_id=0, has_side_effects=True, vmem_limit_bytes=60 << 20),
        name="attend_and_project",
    )(queries, stacked_keys, stacked_values, doc_start.reshape(CHUNKS, CHUNK), out_weight)


def solution(mesh):
    from jax.sharding import PartitionSpec as P

    return jax.shard_map(
        local,
        mesh=mesh,
        in_specs=(P("ctx", "tp"), P("ctx", "tp"), P("ctx", "tp"), P("ctx"), P("tp", None)),
        out_specs=P("ctx", "tp"),
        check_vma=False,
    )
```

time: 430 us -> 101 us (0.23)
  starting transfers between devices: 192 us -> 0 us
  waiting for transfers between devices: 163 us -> 0 us
  Pallas kernels: 0 us -> 98.9 us
  local copies, waits for them, and re-layouts: 33.3 us -> 1.87 us
  matrix products: 17.3 us -> 0 us
  between operations: 13.5 us -> 0.01 us
  loops' own time: 10.6 us -> 0 us
    ppermute x32 -> x0, starting transfers between devices: 192 us -> none  [shifted(): return lax.ppermute(block, axis, route)]
    reduce_scatter x1 -> x0, waiting for transfers between devices: 154 us -> none  [local(): lax.psum_scatter(partial_value.astype(jnp.bfloat16), 'tp', scatter_dimens...]
    pallas_call x0 -> x1, Pallas kernels: none -> 98.9 us  [local(): pl.pallas_call(kernel, out_shape=jax.ShapeDtypeStruct((ROWS, COLS), BF16)...]
    while x33 -> x0, local copies, waits for them, and re-layouts: 22.8 us -> none
    dot_general x3 -> x0, matrix products: 17.3 us -> none  [the longest x1 9.5 us: local(): jnp.dot(attended, out_weight, preferred_element_type=jnp.float32)]
    another operation x17 -> x0, loops' own time: 10.6 us -> none  [the longest x1 10.6 us: local(): lax.fori_loop(1, reach + 1, relay_step, (state, stacked_keys, stacked_val...]
    ppermute x32 -> x0, waiting for transfers between devices: 8.45 us -> none  [shifted(): return lax.ppermute(block, axis, route)]
    unnamed x12 -> x1, local copies, waits for them, and re-layouts: 9.21 us -> 1.87 us
  transfers between devices with their start and end apart: 33 -> 0, of which waited for: 17 -> 0; matrix products, arithmetic and copies ran while one was open for 0% -> 0% of each run, Pallas kernels for 0% -> 0%
where the time goes in v1:
time: 101 us
  Pallas kernels  98.9 us (98%)
  local copies, waits for them, and re-layouts  1.87 us (2%)
    pallas_call x1, Pallas kernels, local(): pl.pallas_call(kernel, out_shape=jax.ShapeDtypeStruct((ROWS, COLS), BF16)...  98.9 us

profile of v1, /device:TPU:2, one launch (start us, length us, event | category | flops | bytes accessed | tf_op | source)
XLA Modules:
  0.0 100.8 jit_solution(1829440547626873155)
XLA Ops:
  0.0 98.9 %attend_and_project.1 = bf16[512,512]{1,0:T(8,128)(2,1)} custom-call(bf16[512,1024]{1,0:T(8,128)(2,1)} %q_hbm.1, bf16[512,128]{1,0:T(8,128)(2,1)} %k_ref.1, bf16[512,128]{1,0:T(8,128)(2,1)} %v_ref.1, s32[4,128]{1,0:T(4,128)} %bitcast.1, bf16[1024,4096]{1,0:T(8,128)(2,1)} %w_hbm.1), custom_call_target="tpu_custom_call" | custom-call | tf_op jit(solution)/shard_map/attend_and_project/pallas_call | solution.py:330
  98.9 1.9 %copy.7 = bf16[512,512]{1,0:T(8,128)(2,1)} copy(bf16[512,512]{1,0:T(8,128)(2,1)} %attend_and_project.1) | data formatting | bytes 1048576

commit v2 on v1

--- a/solution.py
+++ b/solution.py
@@ -68,22 +68,20 @@
         off = pl.multiple_of(h * ROWS, ROWS)
         return kb.at[slot, pl.ds(off, ROWS), :], vb.at[slot, :, pl.ds(off, ROWS)]
 
-    def message(src, slot, h, number, mate):
-        dst = half(slot, h)
-        return [
-            pltpu.make_async_remote_copy(
-                src_ref=src[n], dst_ref=dst[n], send_sem=kv_send.at[2 * number + n],
-                recv_sem=kv_recv.at[2 * number + n], device_id=mate, device_id_type=MESH)
-            for n in range(2)
-        ]
+    def part_copy(src, slot, h, number, mate, n):
+        return pltpu.make_async_remote_copy(
+            src_ref=src[n], dst_ref=half(slot, h)[n], send_sem=kv_send.at[2 * number + n],
+            recv_sem=kv_recv.at[2 * number + n], device_id=mate, device_id_type=MESH)
+
+    def send_part(src, slot, h, number, mate, n):
+        part_copy(src, slot, h, number, mate, n).start()
 
     def send(src, slot, h, number, mate):
-        for copy in message(src, slot, h, number, mate):
-            copy.start()
-
-    def arrived(slot, h, number):
-        for copy in message(half(slot, h), slot, h, number, core):
-            copy.wait_recv()
+        for n in range(2):
+            send_part(src, slot, h, number, mate, n)
+
+    def arrived(slot, h, number, n):
+        part_copy(half(slot, h), slot, h, number, core, n).wait_recv()
 
     own = (k_own, v_own)
     send(own, yl, c, 0, z_next)
@@ -97,38 +95,40 @@
         send(own, 6, 0, 7, core)
 
     def relay(dz):
-        if dz == 4:
-            arrived(6, c, 3)
-
-            @pl.when(c == 1)
-            def _():
-                send(half(6, 1), 6, 1, 7, core)
-
-            @pl.when(yl == 1)
-            def _():
-                send(half(6, c), 7, c, 11, y_mate)
-            return
-        slot = 2 * (dz - 1) + yl
-        arrived(slot, c, dz - 1)
-        src = half(slot, c)
-        send(src, 6 if dz == 3 else slot + 2, c, dz, z_next)
-        send(src, slot, c, 3 + dz, core)
-        send(src, slot, c, 7 + dz, y_mate)
+        for n in range(2):
+            if dz == 4:
+                arrived(6, c, 3, n)
+
+                @pl.when(c == 1)
+                def _(n=n):
+                    send_part(half(6, 1), 6, 1, 7, core, n)
+
+                @pl.when(yl == 1)
+                def _(n=n):
+                    send_part(half(6, c), 7, c, 11, y_mate, n)
+                continue
+            slot = 2 * (dz - 1) + yl
+            arrived(slot, c, dz - 1, n)
+            src = half(slot, c)
+            send_part(src, 6 if dz == 3 else slot + 2, c, dz, z_next, n)
+            send_part(src, slot, c, 3 + dz, core, n)
+            send_part(src, slot, c, 7 + dz, y_mate, n)
 
     def relay_y(dz):
         slot = 7 if dz == 4 else 2 * (dz - 1) + 1 - yl
-        arrived(slot, c, 7 + dz)
-        send(half(slot, c), slot, c, 11 + dz, core)
-
-    def ready(step):
+        for n in range(2):
+            arrived(slot, c, 7 + dz, n)
+            send_part(half(slot, c), slot, c, 11 + dz, core, n)
+
+    def ready(step, n):
         if step == 6:
-            arrived(6, 1 - c, 7)
+            arrived(6, 1 - c, 7, n)
         elif step == 7:
-            arrived(7, 1 - c, 15)
+            arrived(7, 1 - c, 15, n)
         elif step % 2 == 0:
-            arrived(step + yl, 1 - c, 4 + step // 2)
+            arrived(step + yl, 1 - c, 4 + step // 2, n)
         else:
-            arrived(step - yl, 1 - c, 12 + step // 2)
+            arrived(step - yl, 1 - c, 12 + step // 2, n)
 
     def slot_of(step):
         b = step % 2
@@ -195,7 +195,7 @@
         acc[:, cols] = acc[:, cols] * jnp.exp2(m_old - m) + new
 
     relay(1)
-    ready(0)
+    ready(0, 0)
     scores(slot_of(0), 0, 0)
 
     steps = 8 - TAIL
@@ -212,7 +212,11 @@
                     relay_y(n + 1)
                 if n <= 2:
                     relay(n + 2)
-                ready(n + 1)
+                ready(n + 1, 0)
+
+            @pl.when(hs == 2 * n)
+            def _(n=n):
+                ready(n, 1)
 
         slot = slot_of(step)
         ends = ends_of(step)
@@ -282,10 +286,14 @@
             step = 8 - TAIL + n
             if n < TAIL - 1:
                 @pl.when(r == 0)
-                def _():
-                    ready(step + 1)
+                def _(step=step):
+                    ready(step, 1)
+                    ready(step + 1, 0)
                 scores(tail_step(step + 1)[0], r, (n + 1) % 2)
             else:
+                @pl.when(r == 0)
+                def _(step=step):
+                    ready(step, 1)
                 scores(tail_step(8 - TAIL)[0], (r + 1) % CHUNKS, 0)
             slot, ends = tail_step(step)
             update(slot, r, n % 2, ends)
@@ -298,11 +306,13 @@
         done = (acc[0:HEAD, cols] / acc[HEAD:HEAD + 1, cols]).astype(BF16)
         for h in range(HEADS):
             att[:, h * HEAD:(h + 1) * HEAD] = done[:, h * CHUNK:(h + 1) * CHUNK].T
-        for block in range(8):
-            part[r, block] = jnp.dot(att[...], w_buf[:, block * COLS:(block + 1) * COLS],
+        for n, step in enumerate((1, 0, 2, 3, 4, 5, 6, 7)):
+            block = (2 * far + step) % 8
+            at = pl.multiple_of(block * COLS, COLS)
+            part[r, block] = jnp.dot(att[...], w_buf[:, pl.ds(at, COLS)],
                                      preferred_element_type=F32).astype(BF16)
-        for copy in first(r):
-            copy.start()
+            if n < 2:
+                first(r)[n].start()
 
         @pl.when(r >= 2)
         def _():
@@ -317,8 +327,8 @@
     pass_third(3)
 
     for number in range(16):
-        for copy in message(own, 0, 0, number, core):
-            copy.wait_send()
+        for n in range(2):
+            part_copy(own, 0, 0, number, core, n).wait_send()
     for r in range(CHUNKS):
         for copy in (*first(r), *second(r), third(r)):
             copy.wait_send()

time: 101 us -> 100 us (0.990)
  no operation moved by 1% of the time
where the time goes in v2:
time: 100 us
  Pallas kernels  98.2 us (98%)
  local copies, waits for them, and re-layouts  1.87 us (2%)
    pallas_call x1, Pallas kernels, local(): pl.pallas_call(kernel, out_shape=jax.ShapeDtypeStruct((ROWS, COLS), BF16)...  98.2 us

profile of v2, /device:TPU:2, one launch (start us, length us, event | category | flops | bytes accessed | tf_op | source)
XLA Modules:
  0.0 100.1 jit_solution(9235193877540504088)
XLA Ops:
  0.0 98.2 %attend_and_project.1 = bf16[512,512]{1,0:T(8,128)(2,1)} custom-call(bf16[512,1024]{1,0:T(8,128)(2,1)} %q_hbm.1, bf16[512,128]{1,0:T(8,128)(2,1)} %k_ref.1, bf16[512,128]{1,0:T(8,128)(2,1)} %v_ref.1, s32[4,128]{1,0:T(4,128)} %bitcast.1, bf16[1024,4096]{1,0:T(8,128)(2,1)} %w_hbm.1), custom_call_target="tpu_custom_call" | custom-call | tf_op jit(solution)/shard_map/attend_and_project/pallas_call | solution.py:340
  98.2 1.9 %copy.7 = bf16[512,512]{1,0:T(8,128)(2,1)} copy(bf16[512,512]{1,0:T(8,128)(2,1)} %attend_and_project.1) | data formatting | bytes 1048576
